TPU v7x, 256 devices: a whole 4x4x8 slice. The times are simulated.
256 devices in a mesh: row: 16 (over y_lo, x, core), col: 16 (over z, y_hi).
Axes of the slice: x: 4, y: 4 (y_hi: 2, y_lo: 2; y = y_hi * 2 + y_lo), z: 8, core: 2. Of those that a mesh axis runs over, the one named last changes fastest.
Arguments:
- row_frames: float32 [3, 8192, 256], P(None, ('row', 'col')), may hold values from -40 to 40, as said below
- col_frames: float32 [3, 8192, 256], P(None, ('col', 'row')), may hold values from -40 to 40, as said below
- vectors: float32 [64, 8192], P(None, ('col', 'row')), may hold values from -6 to 6
Outputs:
- embedding_product: float32 [64, 8192], P(None, ('row', 'col'))
Inputs may be any that keep to these rules, and one draw needn't show every extreme that they name: `row_frames`: frames of one chain of 256 atoms, each rigidly rotated and moved and perturbed by its own amount. `col_frames`: frames of one chain of 256 atoms, each rigidly rotated and moved and perturbed by its own amount.
All inputs are finite; a program needn't handle non-finite values.
Results may differ from a plain program's by a relative error of at most 0.00017.
Values sent between devices are 32-bit elements; how exact they have to be, the bound alone decides.
A program may use at most 64 MiB of HBM per device.

v0:
```python
import jax
import jax.numpy as jnp
from jax import lax
from jax.sharding import PartitionSpec as P

NEWTON = 8


band_width = 2.0


def centre(frames):
    return frames - jnp.mean(frames, axis=2, keepdims=True)


def kernel_tile(rows, cols):
    count_rows = rows.shape[1]
    count_cols = cols.shape[1]
    atoms = rows.shape[2]
    row_norms = jnp.sum(rows * rows, axis=(0, 2))
    col_norms = jnp.sum(cols * cols, axis=(0, 2))
    product = jnp.dot(
        cols.reshape(3 * count_cols, atoms),
        rows.reshape(3 * count_rows, atoms).T,
        precision=lax.Precision.HIGHEST,
        preferred_element_type=jnp.float32,
    )
    product = product.reshape(3, count_cols, 3, count_rows)
    moment = [[product[second, :, first, :] for second in range(3)] for first in range(3)]
    half_norm = 0.5 * (row_norms[None, :] + col_norms[:, None])
    coef_two = -2.0 * sum(
        (moment[first][second] * moment[first][second] for first in range(3) for second in range(3))
    )
    coef_one = 8.0 * (
        moment[0][0] * moment[1][2] * moment[2][1]
        + moment[1][1] * moment[2][0] * moment[0][2]
        + moment[2][2] * moment[0][1] * moment[1][0]
    ) - 8.0 * (
        moment[0][0] * moment[1][1] * moment[2][2]
        + moment[1][2] * moment[2][0] * moment[0][1]
        + moment[2][1] * moment[1][0] * moment[0][2]
    )
    trace_one = moment[0][0] + moment[1][1] + moment[2][2]
    key_matrix = [
        [
            trace_one,
            moment[1][2] - moment[2][1],
            moment[2][0] - moment[0][2],
            moment[0][1] - moment[1][0],
        ],
        [
            moment[1][2] - moment[2][1],
            moment[0][0] - moment[1][1] - moment[2][2],
            moment[0][1] + moment[1][0],
            moment[2][0] + moment[0][2],
        ],
        [
            moment[2][0] - moment[0][2],
            moment[0][1] + moment[1][0],
            -moment[0][0] + moment[1][1] - moment[2][2],
            moment[1][2] + moment[2][1],
        ],
        [
            moment[0][1] - moment[1][0],
            moment[2][0] + moment[0][2],
            moment[1][2] + moment[2][1],
            -moment[0][0] - moment[1][1] + moment[2][2],
        ],
    ]
    minor_top = [
        key_matrix[0][0] * key_matrix[1][1] - key_matrix[1][0] * key_matrix[0][1],
        key_matrix[0][0] * key_matrix[1][2] - key_matrix[1][0] * key_matrix[0][2],
        key_matrix[0][0] * key_matrix[1][3] - key_matrix[1][0] * key_matrix[0][3],
        key_matrix[0][1] * key_matrix[1][2] - key_matrix[1][1] * key_matrix[0][2],
        key_matrix[0][1] * key_matrix[1][3] - key_matrix[1][1] * key_matrix[0][3],
        key_matrix[0][2] * key_matrix[1][3] - key_matrix[1][2] * key_matrix[0][3],
    ]
    minor_low = [
        key_matrix[2][0] * key_matrix[3][1] - key_matrix[3][0] * key_matrix[2][1],
        key_matrix[2][0] * key_matrix[3][2] - key_matrix[3][0] * key_matrix[2][2],
        key_matrix[2][0] * key_matrix[3][3] - key_matrix[3][0] * key_matrix[2][3],
        key_matrix[2][1] * key_matrix[3][2] - key_matrix[3][1] * key_matrix[2][2],
        key_matrix[2][1] * key_matrix[3][3] - key_matrix[3][1] * key_matrix[2][3],
        key_matrix[2][2] * key_matrix[3][3] - key_matrix[3][2] * key_matrix[2][3],
    ]
    coef_zero = (
        minor_top[0] * minor_low[5]
        - minor_top[1] * minor_low[4]
        + minor_top[2] * minor_low[3]
        + minor_top[3] * minor_low[2]
        - minor_top[4] * minor_low[1]
        + minor_top[5] * minor_low[0]
    )
    eigen = half_norm
    for newton_step in range(NEWTON):
        eigen_sq = eigen * eigen
        value = (eigen_sq + coef_two) * eigen_sq + coef_one * eigen + coef_zero
        slope = 4.0 * eigen_sq * eigen + 2.0 * coef_two * eigen + coef_one
        eigen = eigen - value / slope
    squared = jnp.maximum(2.0 * (half_norm - eigen) / atoms, 0.0)
    return jnp.exp(-squared / band_width)


def per_device(row_frames, col_frames, vectors):
    rows_own = centre(row_frames)
    cols_own = centre(col_frames)
    panel_rows = lax.all_gather(rows_own, "col", axis=1, tiled=True)
    tile = kernel_tile(panel_rows, lax.all_gather(cols_own, "row", axis=1, tiled=True))
    weighted = jnp.dot(
        lax.all_gather(vectors, "row", axis=1, tiled=True),
        tile,
        precision=lax.Precision.HIGHEST,
        preferred_element_type=jnp.float32,
    )
    degree = jnp.sum(tile, axis=0, keepdims=True)
    summed, total = (
        lax.psum_scatter(weighted, "col", scatter_dimension=1, tiled=True),
        lax.psum_scatter(degree, "col", scatter_dimension=1, tiled=True),
    )
    return summed / total


def solution(mesh):
    return jax.shard_map(
        per_device,
        mesh=mesh,
        in_specs=(
            P(None, ("row", "col"), None),
            P(None, ("col", "row"), None),
            P(None, ("col", "row")),
        ),
        out_specs=P(None, ("row", "col")),
        check_vma=False,
    )
```

profile of v0, /device:TPU:1, one launch (start us, length us, event | category | flops | bytes accessed | tf_op | source)
XLA Modules:
  0.0 554.7 jit_solution(16649390457122390750)
XLA Ops:
  6.5 0.0 all-gather.5.cloned.1.call-start
  6.5 1.0 reduce_sum.47
  7.5 1.6 broadcast_subtract_fusion
  9.1 0.0 all-gather.5.cloned.1.call-update
  9.2 0.0 all-gather.3.cloned.1.call-start
  9.2 1.0 reduce_sum.45
  10.2 1.6 broadcast_subtract_fusion.1
  11.8 0.0 all-gather.3.cloned.1.call-update
  11.8 0.0 reduce-scatter.9.cloned.1.call-start
  11.9 22.0 %all_gather.11 = f32[64,512]{0,1:T(8,128)S(1)} all-gather(f32[64,32]{0,1:T(8,128)} %param.5), channel_id=1, replica_groups=mesh['row'=16,'col'=16] {'row'}, dimensions={1}, use_global_device_ids=true | all-gather | bytes 139264 | tf_op jit(solution)/shard_map/all_gather | solution.py:110
  33.9 15.3 %all-gather.5.cloned.1.call-done = f32[3,512,256]{2,1,0:T(8,128)} async-done(((f32[3,32,256]{2,1,0:T(8,128)}), f32[3,512,256]{2,1,0:T(8,128)}) %all-gather.5.cloned.1.call-update) | async-done | bytes 1572880 | tf_op jit(solution)/shard_map/all_gather | solution.py:108
  49.2 0.0 copy-start
  49.2 1.7 multiply_reduce_fusion
  50.9 79.6 %all-gather.3.cloned.1.call-done = f32[3,512,256]{2,1,0:T(8,128)} async-done(((f32[3,32,256]{2,1,0:T(8,128)}), f32[3,512,256]{2,1,0:T(8,128)}) %all-gather.3.cloned.1.call-update) | async-done | bytes 1572880 | tf_op jit(solution)/shard_map/all_gather | solution.py:107
  130.5 0.0 copy-done
  130.5 0.0 copy-start.1
  130.5 9.8 %fusion = f32[3,512,3,512]{3,1,2,0:T(8,128)S(1)} fusion(f32[3,512,256]{2,1,0:T(8,128)S(1)} %copy-done, f32[3,512,256]{2,1,0:T(8,128)} %all-gather.3.cloned.1.call-done), kind=kOutput, calls=%fused_computation | convolution fusion | flops 7247757312 | bytes 12582912 | tf_op jit(solution)/shard_map/dot_general | solution.py:22
  140.3 0.0 copy-done.1
  140.3 0.2 multiply_reduce_fusion.1
  140.5 8.1 %fusion.42 = (f32[512]{0:T(512)S(1)}, f32[512,512]{1,0:T(8,128)S(1)}) fusion(f32[3,512,3,512]{3,1,2,0:T(8,128)S(1)} %fusion, f32[512]{0:T(512)S(1)} %multiply_reduce_fusion, f32[512]{0:T(512)S(1)} %multiply_reduce_fusion.1), kind=kLoop, calls=%fused_computation.77 | loop fusion | flops 52690432 | bytes 10491904 | tf_op jit(solution)/shard_map/reduce_sum | solution.py:115
  148.6 0.9 copy.10
  149.5 0.0 reduce-scatter.9.cloned.1.call-update
  149.5 0.0 reduce-scatter.7.cloned.1.call-start
  149.5 0.8 convolution_bitcast_fusion
  150.3 0.8 copy.8
  151.1 0.0 reduce-scatter.7.cloned.1.call-update
  151.2 193.4 %reduce-scatter.9.cloned.1.call-done = f32[32,1]{1,0:T(8,128)} async-done(((f32[512,1]{1,0:T(8,128)}), f32[32,1]{1,0:T(8,128)}) %reduce-scatter.9.cloned.1.call-update) | async-done | bytes 144
  344.6 0.8 copy.11
  345.3 201.4 %reduce-scatter.7.cloned.1.call-done = f32[32,64]{1,0:T(8,128)} async-done(((f32[512,64]{1,0:T(8,128)}), f32[32,64]{1,0:T(8,128)}) %reduce-scatter.7.cloned.1.call-update) | async-done | bytes 8208
  546.7 1.4 bitcast_divide_fusion
  (2 shorter events, 0.0 us)
Async XLA Ops:
  6.5 42.6 %all-gather.5.cloned.1.call-start = ((), (), s32[]{:S(2)}) async-start(), calls=%async_computation.3 | async-start | bytes 1671168 | tf_op jit(solution)/shard_map/all_gather | solution.py:108
  9.2 121.3 %all-gather.3.cloned.1.call-start = ((), (), s32[]{:S(2)}) async-start(), calls=%async_computation.2 | async-start | bytes 1671168 | tf_op jit(solution)/shard_map/all_gather | solution.py:107
  11.8 332.7 %reduce-scatter.9.cloned.1.call-start = ((), (), s32[]{:S(2)}) async-start(), calls=%async_computation.5 | async-start | bytes 278528
  49.2 81.3 %copy-start = (f32[3,512,256]{2,1,0:T(8,128)S(1)}, f32[3,512,256]{2,1,0:T(8,128)}, u32[]{:S(2)}) copy-start(f32[3,512,256]{2,1,0:T(8,128)} %all-gather.5.cloned.1.call-done) | copy-start | bytes 4718596
  130.5 9.8 %copy-start.1 = (f32[3,512,256]{2,1,0:T(8,128)S(1)}, f32[3,512,256]{2,1,0:T(8,128)}, u32[]{:S(2)}) copy-start(f32[3,512,256]{2,1,0:T(8,128)} %all-gather.3.cloned.1.call-done) | copy-start | bytes 4718596
  149.5 397.2 %reduce-scatter.7.cloned.1.call-start = ((), (), s32[]{:S(2)}) async-start(), calls=%async_computation.4 | async-start | bytes 278528
Sparse Core Ops, SparseCore 0:
  9.3 39.8 all-gather.4
  51.7 78.6 all-gather.2
  149.6 194.8 reduce-scatter.8
  348.7 198.0 reduce-scatter.6
where the time goes:
time: 559 us; the launch traced here: 555 us
  waiting for transfers between devices  490 us (88%)
  blocking collectives  22 us (4%)
  other arithmetic  16.6 us (3%)
  between operations  13.2 us (2%)
  matrix products  10.6 us (2%)
    unnamed x6, waiting for transfers between devices  395 us
    all_gather x1, waiting for transfers between devices, per_device(): panel_rows = lax.all_gather(rows_own, 'col', axis=1, tiled=True)  79.6 us
    all_gather x1, blocking collectives, per_device(): lax.all_gather(vectors, 'row', axis=1, tiled=True)  22 us
    all_gather x1, waiting for transfers between devices, per_device(): lax.all_gather(cols_own, 'row', axis=1, tiled=True)  15.3 us
  transfers between devices with their start and end apart: 4, of which 4 were waited for; matrix products, arithmetic and copies ran while one was open for 1% of the time, Pallas kernels for 0%

commit v1 on v0

v1 whole, which is shorter than its diff:
```python
import jax
import jax.numpy as jnp
from jax import lax
from jax.experimental import pallas as pl
from jax.experimental.pallas import tpu as pltpu
from jax.sharding import PartitionSpec as P

NEWTON = 8
ATOMS = 256
FRAMES = 32
SLICE = 32
MESH = pl.DeviceIdType.MESH

ROW_SLOTS = (
    (0, 0), (1, 0), (3, 0), (0, 1),
    (0, 3), (1, 1), (1, 3), (2, 0),
    (3, 1), (3, 3), (0, 2), (2, 1),
    (2, 3), (1, 2), (3, 2), (2, 2),
)
ROW_AT = {where: at for at, where in enumerate(ROW_SLOTS)}
COL_GROUPS = ((1, 7), (2, 6), (3, 5), (0, 4))


def row_source(slot):
    first, second = slot
    if second == 0:
        source = {1: (0, 0), 3: (0, 0), 2: (1, 0)}[first]
        return source, ((3, 0) if first in (1, 2) else (1, 0))
    if second == 1:
        return (first, 0), (0, 3)
    if second == 3:
        return (first, 0), (0, 1)
    if first < 2:
        return (first, 1), (0, 3)
    return (first, 3), (0, 1)


def split(value):
    high = value.astype(jnp.bfloat16)
    low = (value - high.astype(jnp.float32)).astype(jnp.bfloat16)
    return high, low


def kernel_values(moment, row_norm, col_norm):
    s00, s01, s02, s10, s11, s12, s20, s21, s22 = moment
    cof = (
        s11 * s22 - s12 * s21, s12 * s20 - s10 * s22, s10 * s21 - s11 * s20,
        s02 * s21 - s01 * s22, s00 * s22 - s02 * s20, s01 * s20 - s00 * s21,
        s01 * s12 - s02 * s11, s02 * s10 - s00 * s12, s00 * s11 - s01 * s10,
    )
    total = s00 * s00
    for entry in moment[1:]:
        total = total + entry * entry
    minors = cof[0] * cof[0]
    for entry in cof[1:]:
        minors = minors + entry * entry
    coef_two = -2.0 * total
    coef_one = -8.0 * (s00 * cof[0] + s01 * cof[1] + s02 * cof[2])
    coef_zero = total * total - 4.0 * minors
    half_norm = 0.5 * (row_norm + col_norm)
    eigen = half_norm
    for _ in range(NEWTON):
        square = eigen * eigen
        inner = square + coef_two
        cubic = inner * eigen + coef_one
        value = cubic * eigen + coef_zero
        slope = cubic + eigen * (inner + (square + square))
        eigen = eigen - value / slope
    return jnp.exp(jnp.minimum((eigen - half_norm) * (1.0 / ATOMS), 0.0))


def body(
    rows_ref, cols_ref, vec_ref, out_ref,
    rbuf, cbuf, rsplit, csplit, vsplit, rnorm, cnorm, moments, acc, parts, landed, square_buf,
    rsend, rrecv, csend, crecv, psend, precv, ssend, srecv,
):
    row, col = lax.axis_index("row"), lax.axis_index("col")
    core = lax.rem(row, 2)
    at_x = lax.rem(lax.div(row, 2), 4)
    at_y = lax.rem(col, 2) * 2 + lax.div(row, 8)
    at_z = lax.div(col, 2)

    def device(first, second, along=0, other=False):
        to_x = lax.rem(at_x + (1 - core) * first + core * (4 - second), 4)
        to_y = lax.rem(at_y + (1 - core) * second + core * (4 - first), 4)
        to_z = lax.rem(at_z + (1 - core) * along + core * (8 - along), 8)
        to_core = 1 - core if other else core
        to_row = (lax.rem(to_y, 2) * 4 + to_x) * 2 + to_core
        return (to_row, to_z * 2 + lax.div(to_y, 2))

    neighbours = (
        device(1, 0), device(3, 0), device(0, 1), device(0, 3),
        device(0, 0, 1), device(0, 0, 7), device(0, 0, 0, True),
    )
    barrier = pltpu.get_barrier_semaphore()
    for neighbour in neighbours:
        pl.semaphore_signal(barrier, inc=1, device_id=neighbour, device_id_type=MESH)

    def row_copy(slot):
        source, toward = row_source(slot)
        at = ROW_AT[slot]
        return pltpu.make_async_remote_copy(
            src_ref=rbuf.at[ROW_AT[source]], dst_ref=rbuf.at[at],
            send_sem=rsend.at[at], recv_sem=rrecv.at[at],
            device_id=device(*toward), device_id_type=MESH,
        )

    def col_copy(slot):
        source, toward = (slot - 1, 7) if slot <= 4 else ((slot + 1) % 8, 1)
        return pltpu.make_async_remote_copy(
            src_ref=cbuf.at[0, source], dst_ref=cbuf.at[0, slot],
            send_sem=csend.at[slot], recv_sem=crecv.at[slot],
            device_id=device(0, 0, toward), device_id_type=MESH,
        )

    def pair_copy(slot):
        return pltpu.make_async_remote_copy(
            src_ref=cbuf.at[0, slot], dst_ref=cbuf.at[1, slot],
            send_sem=psend.at[slot], recv_sem=precv.at[slot],
            device_id=device(0, 0, 0, True), device_id_type=MESH,
        )

    def share_copy(at):
        return pltpu.make_async_remote_copy(
            src_ref=parts.at[at], dst_ref=landed.at[at],
            send_sem=ssend.at[at], recv_sem=srecv.at[at],
            device_id=device(*ROW_SLOTS[at]), device_id_type=MESH,
        )

    for comp in range(3):
        frames = rows_ref[comp]
        rbuf[0, comp * FRAMES:(comp + 1) * FRAMES, :] = frames - jnp.mean(frames, axis=1, keepdims=True)
        frames = cols_ref[comp]
        cbuf[0, 0, comp * FRAMES:(comp + 1) * FRAMES, :] = frames - jnp.mean(frames, axis=1, keepdims=True)
    square_buf[...] = jnp.zeros_like(square_buf)
    square_buf[0:64, 0:FRAMES] = vec_ref[...]
    square_buf[64:72, :] = jnp.ones((8, 128), jnp.float32)
    turned = square_buf[...].T
    cbuf[0, 0, 96:112, 0:128] = turned[0:16, :]
    cbuf[0, 0, 96:112, 128:256] = turned[16:32, :]
    acc[...] = jnp.zeros_like(acc)

    pl.semaphore_wait(barrier, len(neighbours))

    for slot in ((1, 0), (3, 0), (0, 1), (0, 3)):
        row_copy(slot).start()
    col_copy(1).start()
    col_copy(7).start()
    pair_copy(0).start()

    def prepare_rows(chunk):
        for place in range(4):
            norm = jnp.zeros((FRAMES, 1), jnp.float32)
            for comp in range(3):
                value = rbuf[4 * chunk + place, comp * FRAMES:(comp + 1) * FRAMES, :]
                norm = norm + jnp.sum(value * value, axis=1, keepdims=True)
                high, low = split(value)
                at = pl.ds(comp * 128 + place * FRAMES, FRAMES)
                rsplit[chunk, at, 0:256] = high
                rsplit[chunk, at, 256:512] = high
                rsplit[chunk, at, 512:768] = low
            rnorm[chunk, place * FRAMES:(place + 1) * FRAMES, :] = jnp.broadcast_to(norm, (FRAMES, 128))

    def prepare_cols(group):
        for place in range(4):
            kind, slot = place // 2, COL_GROUPS[group][place % 2]
            norm = jnp.zeros((FRAMES, 1), jnp.float32)
            for comp in range(3):
                value = cbuf[kind, slot, comp * FRAMES:(comp + 1) * FRAMES, :]
                norm = norm + jnp.sum(value * value, axis=1, keepdims=True)
                high, low = split(value)
                at = pl.ds(comp * 128 + place * FRAMES, FRAMES)
                csplit[group, at, 0:256] = high
                csplit[group, at, 256:512] = low
                csplit[group, at, 512:768] = high
            square_buf[place * FRAMES:(place + 1) * FRAMES, :] = jnp.broadcast_to(norm, (FRAMES, 128))
            for half in range(2):
                value = cbuf[kind, slot, 96:112, half * 128:(half + 1) * 128]
                high, low = split(value)
                start = place * FRAMES + half * 16
                vsplit[group, start:start + 16, :] = high
                vsplit[group, 128 + start:128 + start + 16, :] = high
                vsplit[group, 256 + start:256 + start + 16, :] = low
        cnorm[group] = square_buf[...].T[0:8, :]

    def unit(chunk, group):
        moments[...] = lax.dot_general(
            rsplit[chunk], csplit[group], (((1,), (1,)), ((), ())),
            preferred_element_type=jnp.float32,
        )
        col_norm = cnorm[group][0:1, :]
        for start in range(0, 128, SLICE):
            moment = [
                moments[first * 128 + start:first * 128 + start + SLICE, second * 128:(second + 1) * 128]
                for first in range(3) for second in range(3)
            ]
            values = kernel_values(moment, rnorm[chunk, start:start + SLICE, :], col_norm)
            high, low = split(values)
            joined = jnp.concatenate([high, low, high], axis=1)
            at = pl.ds(start, SLICE)
            acc[chunk, at, :] = acc[chunk, at, :] + jnp.dot(
                joined, vsplit[group], preferred_element_type=jnp.float32
            )

    def units(count, which):
        def step(index, carry):
            unit(*which(index))
            return carry
        lax.fori_loop(0, count, step, 0)

    def share(chunk):
        for place in range(4):
            at = 4 * chunk + place
            value = acc[chunk, place * FRAMES:(place + 1) * FRAMES, :]
            if at == 0:
                landed[0] = value
            else:
                parts[at] = value
                share_copy(at).start()

    col_copy(1).wait_recv()
    col_copy(2).start()
    pair_copy(1).start()
    col_copy(7).wait_recv()
    col_copy(6).start()
    pair_copy(7).start()
    row_copy((1, 0)).wait_recv()
    for slot in ((2, 0), (1, 1), (1, 3)):
        row_copy(slot).start()
    row_copy((3, 0)).wait_recv()
    for slot in ((3, 1), (3, 3)):
        row_copy(slot).start()
    row_copy((0, 1)).wait_recv()
    row_copy((0, 2)).start()
    prepare_rows(0)
    pair_copy(1).wait_recv()
    pair_copy(7).wait_recv()
    prepare_cols(0)
    units(1, lambda index: (0, 0))

    col_copy(2).wait_recv()
    col_copy(3).start()
    pair_copy(2).start()
    col_copy(6).wait_recv()
    col_copy(5).start()
    pair_copy(6).start()
    row_copy((2, 0)).wait_recv()
    for slot in ((2, 1), (2, 3)):
        row_copy(slot).start()
    row_copy((1, 1)).wait_recv()
    row_copy((1, 2)).start()
    row_copy((3, 3)).wait_recv()
    row_copy((3, 2)).start()
    row_copy((0, 3)).wait_recv()
    row_copy((1, 3)).wait_recv()
    prepare_rows(1)
    pair_copy(2).wait_recv()
    pair_copy(6).wait_recv()
    prepare_cols(1)
    units(3, lambda index: (jnp.minimum(index, 1), jnp.minimum(2 - index, 1)))

    col_copy(3).wait_recv()
    col_copy(4).start()
    pair_copy(3).start()
    col_copy(5).wait_recv()
    pair_copy(5).start()
    row_copy((2, 3)).wait_recv()
    row_copy((2, 2)).start()
    for slot in ((3, 1), (0, 2), (2, 1)):
        row_copy(slot).wait_recv()
    prepare_rows(2)
    pair_copy(3).wait_recv()
    pair_copy(5).wait_recv()
    prepare_cols(2)
    units(5, lambda index: (jnp.minimum(index, 2), jnp.minimum(4 - index, 2)))

    col_copy(4).wait_recv()
    pair_copy(4).start()
    for slot in ((1, 2), (3, 2), (2, 2)):
        row_copy(slot).wait_recv()
    prepare_rows(3)
    pair_copy(0).wait_recv()
    pair_copy(4).wait_recv()
    prepare_cols(3)
    units(4, lambda index: (3, index))
    share(3)
    for chunk in (2, 1, 0):
        units(1, lambda index, chunk=chunk: (chunk, 3))
        share(chunk)

    for slot in ROW_SLOTS[1:]:
        row_copy(slot).wait_send()
    for slot in range(1, 8):
        col_copy(slot).wait_send()
    for slot in range(8):
        pair_copy(slot).wait_send()
    total = landed[0]
    for at in range(15, 0, -1):
        share_copy(at).wait_recv()
        total = total + landed[at]
    square_buf[0:FRAMES, :] = total / total[:, 64:65]
    out_ref[...] = square_buf[...].T[0:64, 0:FRAMES]
    for at in range(1, 16):
        share_copy(at).wait_send()


def per_device(row_frames, col_frames, vectors):
    vmem = pl.BlockSpec(memory_space=pltpu.VMEM)
    dma = pltpu.SemaphoreType.DMA
    return pl.pallas_call(
        body,
        name="qcp_product",
        out_shape=jax.ShapeDtypeStruct(vectors.shape, jnp.float32),
        in_specs=[vmem] * 3,
        out_specs=vmem,
        scratch_shapes=[
            pltpu.VMEM((16, 96, ATOMS), jnp.float32),
            pltpu.VMEM((2, 8, 112, ATOMS), jnp.float32),
            pltpu.VMEM((4, 384, 768), jnp.bfloat16),
            pltpu.VMEM((4, 384, 768), jnp.bfloat16),
            pltpu.VMEM((4, 384, 128), jnp.bfloat16),
            pltpu.VMEM((4, 128, 128), jnp.float32),
            pltpu.VMEM((4, 8, 128), jnp.float32),
            pltpu.VMEM((384, 384), jnp.float32),
            pltpu.VMEM((4, 128, 128), jnp.float32),
            pltpu.VMEM((16, FRAMES, 128), jnp.float32),
            pltpu.VMEM((16, FRAMES, 128), jnp.float32),
            pltpu.VMEM((128, 128), jnp.float32),
            dma((16,)), dma((16,)), dma((8,)), dma((8,)),
            dma((8,)), dma((8,)), dma((16,)), dma((16,)),
        ],
        compiler_params=pltpu.CompilerParams(
            collective_id=0, has_side_effects=True, vmem_limit_bytes=40 << 20,
        ),
    )(row_frames, col_frames, vectors)


def solution(mesh):
    return jax.shard_map(
        per_device,
        mesh=mesh,
        in_specs=(
            P(None, ("row", "col"), None),
            P(None, ("col", "row"), None),
            P(None, ("col", "row")),
        ),
        out_specs=P(None, ("row", "col")),
        check_vma=False,
    )
```

time: 559 us -> 44.9 us (0.08)
  waiting for transfers between devices: 490 us -> 0 us
  Pallas kernels: 0 us -> 41.4 us
  blocking collectives: 22 us -> 0 us
  other arithmetic: 16.6 us -> 0 us
  between operations: 13.2 us -> 0.01 us
  matrix products: 10.6 us -> 0 us
    unnamed x6 -> x0, waiting for transfers between devices: 395 us -> none
    all_gather x2 -> x0, waiting for transfers between devices: 94.9 us -> none  [the longest x1 79.6 us: per_device(): panel_rows = lax.all_gather(rows_own, 'col', axis=1, tiled=True)]
    pallas_call x0 -> x1, Pallas kernels: none -> 41.4 us  [per_device(): pl.pallas_call(body, name='qcp_product', out_shape=jax.ShapeDtypeStruct(v...]
    all_gather x1 -> x0, blocking collectives: 22 us -> none  [per_device(): lax.all_gather(vectors, 'row', axis=1, tiled=True)]
    reduce_sum x5 -> x0, other arithmetic: 12 us -> none  [the longest x1 8.12 us: per_device(): degree = jnp.sum(tile, axis=0, keepdims=True)]
    dot_general x2 -> x0, matrix products: 10.6 us -> none  [the longest x1 9.78 us: kernel_tile(): jnp.dot(cols.reshape(3 * count_cols, atoms), rows.reshape(3 * count_rows,...]
  transfers between devices with their start and end apart: 4 -> 0, of which waited for: 4 -> 0; matrix products, arithmetic and copies ran while one was open for 1% -> 0% of each run, Pallas kernels for 0% -> 0%
where the time goes in v1:
time: 44.9 us; the launch traced here: 44.7 us
  Pallas kernels  41.4 us (92%)
  local copies, waits for them, and re-layouts  3.26 us (7%)
    pallas_call x1, Pallas kernels, per_device(): pl.pallas_call(body, name='qcp_product', out_shape=jax.ShapeDtypeStruct(v...  41.4 us
    unnamed x5, local copies, waits for them, and re-layouts  2.58 us

profile of v1, /device:TPU:1, one launch (start us, length us, event | category | flops | bytes accessed | tf_op | source)
XLA Modules:
  0.0 44.7 jit_solution(15469971089598348383)
XLA Ops:
  0.0 0.8 %copy.4.vec_ref = f32[64,32]{1,0:T(8,128)S(1)} copy(f32[64,32]{0,1:T(8,128)} %param.5) | data formatting | bytes 16384 | tf_op args[2]
  0.8 0.0 copy-start
  0.8 0.9 %copy-done = f32[3,32,256]{2,1,0:T(8,128)S(1)} copy-done((f32[3,32,256]{2,1,0:T(8,128)S(1)}, f32[3,32,256]{2,1,0:T(8,128)}, u32[]{:S(2)}) %copy-start) | copy-done | bytes 98328
  1.7 0.0 copy-start.1
  1.7 0.9 %copy-done.1 = f32[3,32,256]{2,1,0:T(8,128)S(1)} copy-done((f32[3,32,256]{2,1,0:T(8,128)S(1)}, f32[3,32,256]{2,1,0:T(8,128)}, u32[]{:S(2)}) %copy-start.1) | copy-done | bytes 98328
  2.6 41.4 %qcp_product.1 = f32[64,32]{1,0:T(8,128)S(1)} custom-call(f32[3,32,256]{2,1,0:T(8,128)S(1)} %copy-done, f32[3,32,256]{2,1,0:T(8,128)S(1)} %copy-done.1, f32[64,32]{1,0:T(8,128)S(1)} %copy.4.vec_ref), custom_call_target="tpu_custom_call" | custom-call | tf_op jit(solution)/shard_map/qcp_product/pallas_call | solution.py:310
  44.0 0.7 %copy.5 = f32[64,32]{0,1:T(8,128)} copy(f32[64,32]{1,0:T(8,128)S(1)} %qcp_product.1) | data formatting | bytes 16384 | tf_op jit(solution)/shard_map/qcp_product/pallas_call | solution.py:310
Async XLA Ops:
  0.8 0.9 %copy-start = (f32[3,32,256]{2,1,0:T(8,128)S(1)}, f32[3,32,256]{2,1,0:T(8,128)}, u32[]{:S(2)}) copy-start(f32[3,32,256]{2,1,0:T(8,128)} %rows_ref.1) | copy-start | bytes 294916
  1.7 0.9 %copy-start.1 = (f32[3,32,256]{2,1,0:T(8,128)S(1)}, f32[3,32,256]{2,1,0:T(8,128)}, u32[]{:S(2)}) copy-start(f32[3,32,256]{2,1,0:T(8,128)} %cols_ref.1) | copy-start | bytes 294916

commit v2 on v1

v2 whole, which is shorter than its diff:
```python
import jax
import jax.numpy as jnp
from jax import lax
from jax.experimental import pallas as pl
from jax.experimental.pallas import tpu as pltpu
from jax.sharding import PartitionSpec as P

NEWTON = 8
ATOMS = 256
FRAMES = 32
SLICE = 32
MESH = pl.DeviceIdType.MESH

ROW_SLOTS = (
    (0, 0), (1, 0), (3, 0), (0, 1),
    (0, 3), (1, 1), (1, 3), (2, 0),
    (3, 1), (3, 3), (0, 2), (2, 1),
    (2, 3), (1, 2), (3, 2), (2, 2),
)
ROW_AT = {where: at for at, where in enumerate(ROW_SLOTS)}
COL_GROUPS = ((1, 7), (2, 6), (3, 5), (0, 4))


def row_source(slot):
    first, second = slot
    if second == 0:
        source = {1: (0, 0), 3: (0, 0), 2: (1, 0)}[first]
        return source, ((3, 0) if first in (1, 2) else (1, 0))
    if second == 1:
        return (first, 0), (0, 3)
    if second == 3:
        return (first, 0), (0, 1)
    if first < 2:
        return (first, 1), (0, 3)
    return (first, 3), (0, 1)


def split(value):
    high = value.astype(jnp.bfloat16)
    low = (value - high.astype(jnp.float32)).astype(jnp.bfloat16)
    return high, low


def kernel_values(moment, row_norm, col_norm):
    s00, s01, s02, s10, s11, s12, s20, s21, s22 = moment
    g00 = s00 * s00 + s10 * s10 + s20 * s20
    g11 = s01 * s01 + s11 * s11 + s21 * s21
    g22 = s02 * s02 + s12 * s12 + s22 * s22
    g01 = s00 * s01 + s10 * s11 + s20 * s21
    g02 = s00 * s02 + s10 * s12 + s20 * s22
    g12 = s01 * s02 + s11 * s12 + s21 * s22
    pair = g11 + g22
    trace = g00 + pair
    minors = g00 * pair + g11 * g22 - (g01 * g01 + g02 * g02 + g12 * g12)
    det = s00 * (s11 * s22 - s12 * s21) + s01 * (s12 * s20 - s10 * s22) + s02 * (s10 * s21 - s11 * s20)
    half_trace = 0.5 * trace
    free = half_trace * half_trace - minors
    det_two = det + det
    full_norm = row_norm + col_norm
    eigen = full_norm
    for _ in range(NEWTON):
        square = eigen * eigen
        upper = (0.75 * square - half_trace) * square - free
        lower = (square - trace) * eigen - det_two
        eigen = upper / lower
    return jnp.exp(jnp.minimum((eigen - full_norm) * (0.5 / ATOMS), 0.0))


ROW_PIECES = ((0, 32), (32, 32), (64, 32))
COL_PIECES = ((0, 32), (32, 32), (64, 48))
UNITS = (
    ((0, 0),),
    ((0, 1), (1, 1), (1, 0)),
    ((0, 2), (1, 2), (2, 2), (2, 1), (2, 0)),
    ((3, 0), (3, 1), (3, 2), (3, 3), (2, 3), (1, 3), (0, 3)),
)


def body(
    rows_hbm, cols_hbm, vec_hbm, out_ref,
    rows_ref, cols_ref, vec_ref,
    rbuf, cbuf, rsplit, csplit, vsplit, rnorm, cnorm, moments_a, moments_b, ksplit_a, ksplit_b,
    acc, parts, landed, square_buf,
    isem, rsend, rrecv, csend, crecv, psend, precv, ssend, srecv,
):
    row, col = lax.axis_index("row"), lax.axis_index("col")
    core = lax.rem(row, 2)
    at_x = lax.rem(lax.div(row, 2), 4)
    at_y = lax.rem(col, 2) * 2 + lax.div(row, 8)
    at_z = lax.div(col, 2)

    def device(first, second, along=0, other=False):
        to_x = lax.rem(at_x + (1 - core) * first + core * (4 - second), 4)
        to_y = lax.rem(at_y + (1 - core) * second + core * (4 - first), 4)
        to_z = lax.rem(at_z + (1 - core) * along + core * (8 - along), 8)
        to_core = 1 - core if other else core
        to_row = (lax.rem(to_y, 2) * 4 + to_x) * 2 + to_core
        return (to_row, to_z * 2 + lax.div(to_y, 2))

    neighbours = (
        device(1, 0), device(3, 0), device(0, 1), device(0, 3),
        device(0, 0, 1), device(0, 0, 7), device(0, 0, 0, True),
    )
    barrier = pltpu.get_barrier_semaphore()
    for neighbour in neighbours:
        pl.semaphore_signal(barrier, inc=1, device_id=neighbour, device_id_type=MESH)
    loads = (
        pltpu.make_async_copy(rows_hbm, rows_ref, isem.at[0]),
        pltpu.make_async_copy(cols_hbm, cols_ref, isem.at[1]),
        pltpu.make_async_copy(vec_hbm, vec_ref, isem.at[2]),
    )
    for load in loads:
        load.start()

    def row_copy(slot, piece):
        source, toward = row_source(slot)
        at, span = ROW_AT[slot], pl.ds(*ROW_PIECES[piece])
        return pltpu.make_async_remote_copy(
            src_ref=rbuf.at[ROW_AT[source], span], dst_ref=rbuf.at[at, span],
            send_sem=rsend.at[at, piece], recv_sem=rrecv.at[at, piece],
            device_id=device(*toward), device_id_type=MESH,
        )

    def col_copy(slot, piece):
        source, toward = (slot - 1, 7) if slot <= 4 else ((slot + 1) % 8, 1)
        span = pl.ds(*COL_PIECES[piece])
        return pltpu.make_async_remote_copy(
            src_ref=cbuf.at[0, source, span], dst_ref=cbuf.at[0, slot, span],
            send_sem=csend.at[slot, piece], recv_sem=crecv.at[slot, piece],
            device_id=device(0, 0, toward), device_id_type=MESH,
        )

    def pair_copy(slot, piece):
        span = pl.ds(*COL_PIECES[piece])
        return pltpu.make_async_remote_copy(
            src_ref=cbuf.at[0, slot, span], dst_ref=cbuf.at[1, slot, span],
            send_sem=psend.at[slot, piece], recv_sem=precv.at[slot, piece],
            device_id=device(0, 0, 0, True), device_id_type=MESH,
        )

    def share_copy(at):
        return pltpu.make_async_remote_copy(
            src_ref=parts.at[at], dst_ref=landed.at[at],
            send_sem=ssend.at[at], recv_sem=srecv.at[at],
            device_id=device(*ROW_SLOTS[at]), device_id_type=MESH,
        )

    square_buf[...] = jnp.zeros_like(square_buf)
    square_buf[64:72, :] = jnp.ones((8, 128), jnp.float32)
    loads[0].wait()
    for comp in range(3):
        frames = rows_ref[comp]
        centred = frames - jnp.mean(frames, axis=1, keepdims=True)
        rbuf[0, comp * FRAMES:(comp + 1) * FRAMES, :] = centred + centred
    loads[1].wait()
    for comp in range(3):
        frames = cols_ref[comp]
        cbuf[0, 0, comp * FRAMES:(comp + 1) * FRAMES, :] = frames - jnp.mean(frames, axis=1, keepdims=True)
    loads[2].wait()
    square_buf[0:64, 0:FRAMES] = vec_ref[...]
    turned = square_buf[...].T
    cbuf[0, 0, 96:112, 0:128] = turned[0:16, :]
    cbuf[0, 0, 96:112, 128:256] = turned[16:32, :]

    pl.semaphore_wait(barrier, len(neighbours))

    for piece in range(3):
        for slot in ((1, 0), (3, 0), (0, 1), (0, 3)):
            row_copy(slot, piece).start()
        col_copy(1, piece).start()
        col_copy(7, piece).start()
        pair_copy(0, piece).start()

    def pass_on(piece, cols, rows):
        for slot, onward in cols:
            col_copy(slot, piece).wait_recv()
            if onward is not None:
                col_copy(onward, piece).start()
            pair_copy(slot, piece).start()
        for slot, onward in rows:
            row_copy(slot, piece).wait_recv()
            for later in onward:
                row_copy(later, piece).start()

    def first_round(piece):
        pass_on(piece, ((1, 2), (7, 6)), (
            ((1, 0), ((2, 0), (1, 1), (1, 3))), ((3, 0), ((3, 1), (3, 3))), ((0, 1), ((0, 2),)),
        ))

    def second_round(piece):
        pass_on(piece, ((2, 3), (6, 5)), (
            ((2, 0), ((2, 1), (2, 3))), ((1, 1), ((1, 2),)), ((3, 3), ((3, 2),)),
        ))

    def third_round(piece):
        pass_on(piece, ((3, 4), (5, None)), (((2, 3), ((2, 2),)),))

    def settle(rows, cols):
        for piece in range(3):
            for slot in rows:
                row_copy(slot, piece).wait_recv()
            for slot in cols:
                pair_copy(slot, piece).wait_recv()

    def prepare_rows(chunk):
        for place in range(4):
            norm = jnp.zeros((FRAMES, 1), jnp.float32)
            for comp in range(3):
                value = rbuf[4 * chunk + place, comp * FRAMES:(comp + 1) * FRAMES, :]
                norm = norm + jnp.sum(value * value, axis=1, keepdims=True)
                high, low = split(value)
                at = pl.ds(comp * 128 + place * FRAMES, FRAMES)
                rsplit[chunk, at, 0:256] = high
                rsplit[chunk, at, 256:512] = high
                rsplit[chunk, at, 512:768] = low
            rnorm[chunk, place * FRAMES:(place + 1) * FRAMES, :] = jnp.broadcast_to(0.25 * norm, (FRAMES, 128))

    def prepare_cols(group):
        for place in range(4):
            kind, slot = place // 2, COL_GROUPS[group][place % 2]
            norm = jnp.zeros((FRAMES, 1), jnp.float32)
            for comp in range(3):
                value = cbuf[kind, slot, comp * FRAMES:(comp + 1) * FRAMES, :]
                norm = norm + jnp.sum(value * value, axis=1, keepdims=True)
                high, low = split(value)
                at = pl.ds(comp * 128 + place * FRAMES, FRAMES)
                csplit[group, at, 0:256] = high
                csplit[group, at, 256:512] = low
                csplit[group, at, 512:768] = high
            square_buf[place * FRAMES:(place + 1) * FRAMES, :] = jnp.broadcast_to(norm, (FRAMES, 128))
            for half in range(2):
                value = cbuf[kind, slot, 96:112, half * 128:(half + 1) * 128]
                high, low = split(value)
                start = place * FRAMES + half * 16
                vsplit[group, start:start + 16, :] = high
                vsplit[group, 128 + start:128 + start + 16, :] = high
                vsplit[group, 256 + start:256 + start + 16, :] = low
        cnorm[group] = square_buf[...].T[0:8, :]

    def share(chunk):
        for place in range(4):
            at = 4 * chunk + place
            value = acc[chunk, place * FRAMES:(place + 1) * FRAMES, :]
            if at == 0:
                landed[0] = value
            else:
                parts[at] = value
                share_copy(at).start()

    moments, ksplit = (moments_a, moments_b), (ksplit_a, ksplit_b)
    started, flight = set(), {"moments": None, "values": None, "count": 0}

    def advance(unit):
        count = flight["count"]
        if unit is not None:
            moments[count % 2][...] = lax.dot_general(
                rsplit[unit[0]], csplit[unit[1]], (((1,), (1,)), ((), ())),
                preferred_element_type=jnp.float32,
            )
        valued = flight["values"]
        if valued is not None:
            chunk, group = valued
            added = jnp.dot(ksplit[count % 2][...], vsplit[group], preferred_element_type=jnp.float32)
            acc[chunk] = acc[chunk] + added if chunk in started else added
            started.add(chunk)
        ready = flight["moments"]
        if ready is not None:
            chunk, group = ready
            held, into = moments[(count + 1) % 2], ksplit[(count + 1) % 2]
            col_norm = cnorm[group][0:1, :]
            for start in range(0, 128, SLICE):
                moment = [
                    held[first * 128 + start:first * 128 + start + SLICE, second * 128:(second + 1) * 128]
                    for first in range(3) for second in range(3)
                ]
                values = kernel_values(moment, rnorm[chunk, start:start + SLICE, :], col_norm)
                high, low = split(values)
                into[start:start + SLICE, 0:128] = high
                into[start:start + SLICE, 128:256] = low
                into[start:start + SLICE, 256:384] = high
        if valued is not None and valued[1] == 3:
            share(valued[0])
        flight["moments"], flight["values"], flight["count"] = unit, ready, count + 1

    for piece in range(3):
        first_round(piece)
    settle((), (1, 7))
    prepare_rows(0)
    prepare_cols(0)
    second_round(0)
    advance(UNITS[0][0])
    second_round(1)
    second_round(2)
    settle(((0, 3), (1, 3)), (2, 6))
    prepare_rows(1)
    prepare_cols(1)
    for piece in range(3):
        advance(UNITS[1][piece])
        third_round(piece)
    settle(((3, 1), (0, 2), (2, 1)), (3, 5))
    prepare_rows(2)
    prepare_cols(2)
    for at, unit in enumerate(UNITS[2]):
        advance(unit)
        if 1 <= at <= 3:
            col_copy(4, at - 1).wait_recv()
            pair_copy(4, at - 1).start()
    settle(((1, 2), (3, 2), (2, 2)), (0, 4))
    prepare_rows(3)
    prepare_cols(3)
    for unit in UNITS[3]:
        advance(unit)
    advance(None)
    advance(None)

    for piece in range(3):
        for slot in ROW_SLOTS[1:]:
            row_copy(slot, piece).wait_send()
        for slot in range(1, 8):
            col_copy(slot, piece).wait_send()
        for slot in range(8):
            pair_copy(slot, piece).wait_send()
    total = landed[0]
    for at in range(15, 0, -1):
        share_copy(at).wait_recv()
        total = total + landed[at]
    square_buf[0:FRAMES, :] = total / total[:, 64:65]
    out_ref[...] = square_buf[...].T[0:64, 0:FRAMES]
    for at in range(1, 16):
        share_copy(at).wait_send()


def per_device(row_frames, col_frames, vectors):
    vmem = pl.BlockSpec(memory_space=pltpu.VMEM)
    dma = pltpu.SemaphoreType.DMA
    return pl.pallas_call(
        body,
        name="qcp_product",
        out_shape=jax.ShapeDtypeStruct(vectors.shape, jnp.float32),
        in_specs=[pl.BlockSpec(memory_space=pl.ANY)] * 3,
        out_specs=vmem,
        scratch_shapes=[
            pltpu.VMEM(row_frames.shape, jnp.float32),
            pltpu.VMEM(col_frames.shape, jnp.float32),
            pltpu.VMEM(vectors.shape, jnp.float32),
            pltpu.VMEM((16, 96, ATOMS), jnp.float32),
            pltpu.VMEM((2, 8, 112, ATOMS), jnp.float32),
            pltpu.VMEM((4, 384, 768), jnp.bfloat16),
            pltpu.VMEM((4, 384, 768), jnp.bfloat16),
            pltpu.VMEM((4, 384, 128), jnp.bfloat16),
            pltpu.VMEM((4, 128, 128), jnp.float32),
            pltpu.VMEM((4, 8, 128), jnp.float32),
            pltpu.VMEM((384, 384), jnp.float32),
            pltpu.VMEM((384, 384), jnp.float32),
            pltpu.VMEM((128, 384), jnp.bfloat16),
            pltpu.VMEM((128, 384), jnp.bfloat16),
            pltpu.VMEM((4, 128, 128), jnp.float32),
            pltpu.VMEM((16, FRAMES, 128), jnp.float32),
            pltpu.VMEM((16, FRAMES, 128), jnp.float32),
            pltpu.VMEM((128, 128), jnp.float32),
            dma((3,)), dma((16, 3)), dma((16, 3)), dma((8, 3)), dma((8, 3)),
            dma((8, 3)), dma((8, 3)), dma((16,)), dma((16,)),
        ],
        compiler_params=pltpu.CompilerParams(
            collective_id=0, has_side_effects=True, vmem_limit_bytes=40 << 20,
        ),
    )(row_frames, col_frames, vectors)


def solution(mesh):
    return jax.shard_map(
        per_device,
        mesh=mesh,
        in_specs=(
            P(None, ("row", "col"), None),
            P(None, ("col", "row"), None),
            P(None, ("col", "row")),
        ),
        out_specs=P(None, ("row", "col")),
        check_vma=False,
    )
```

time: 44.9 us -> 40 us (0.89)
  Pallas kernels: 41.4 us -> 36.5 us
    pallas_call x1, Pallas kernels: 41.4 us -> 36.5 us  [per_device(): pl.pallas_call(body, name='qcp_product', out_shape=jax.ShapeDtypeStruct(v...]
where the time goes in v2:
time: 40 us; the launch traced here: 39.8 us
  Pallas kernels  36.5 us (91%)
  local copies, waits for them, and re-layouts  3.26 us (8%)
    pallas_call x1, Pallas kernels, per_device(): pl.pallas_call(body, name='qcp_product', out_shape=jax.ShapeDtypeStruct(v...  36.5 us
    unnamed x5, local copies, waits for them, and re-layouts  2.58 us

profile of v2, /device:TPU:1, one launch (start us, length us, event | category | flops | bytes accessed | tf_op | source)
XLA Modules:
  0.0 39.8 jit_solution(6643429396910327391)
XLA Ops:
  0.0 0.8 %copy.4.vec_hbm = f32[64,32]{1,0:T(8,128)S(1)} copy(f32[64,32]{0,1:T(8,128)} %param.5) | data formatting | bytes 16384 | tf_op args[2]
  0.8 0.0 copy-start
  0.8 0.9 %copy-done = f32[3,32,256]{2,1,0:T(8,128)S(1)} copy-done((f32[3,32,256]{2,1,0:T(8,128)S(1)}, f32[3,32,256]{2,1,0:T(8,128)}, u32[]{:S(2)}) %copy-start) | copy-done | bytes 98328
  1.7 0.0 copy-start.1
  1.7 0.9 %copy-done.1 = f32[3,32,256]{2,1,0:T(8,128)S(1)} copy-done((f32[3,32,256]{2,1,0:T(8,128)S(1)}, f32[3,32,256]{2,1,0:T(8,128)}, u32[]{:S(2)}) %copy-start.1) | copy-done | bytes 98328
  2.6 36.5 %qcp_product.1 = f32[64,32]{1,0:T(8,128)S(1)} custom-call(f32[3,32,256]{2,1,0:T(8,128)S(1)} %copy-done, f32[3,32,256]{2,1,0:T(8,128)S(1)} %copy-done.1, f32[64,32]{1,0:T(8,128)S(1)} %copy.4.vec_hbm), custom_call_target="tpu_custom_call" | custom-call | tf_op jit(solution)/shard_map/qcp_product/pallas_call | solution.py:336
  39.1 0.7 %copy.5 = f32[64,32]{0,1:T(8,128)} copy(f32[64,32]{1,0:T(8,128)S(1)} %qcp_product.1) | data formatting | bytes 16384 | tf_op jit(solution)/shard_map/qcp_product/pallas_call | solution.py:336
Async XLA Ops:
  0.8 0.9 %copy-start = (f32[3,32,256]{2,1,0:T(8,128)S(1)}, f32[3,32,256]{2,1,0:T(8,128)}, u32[]{:S(2)}) copy-start(f32[3,32,256]{2,1,0:T(8,128)} %rows_hbm.1) | copy-start | bytes 294916
  1.7 0.9 %copy-start.1 = (f32[3,32,256]{2,1,0:T(8,128)S(1)}, f32[3,32,256]{2,1,0:T(8,128)}, u32[]{:S(2)}) copy-start(f32[3,32,256]{2,1,0:T(8,128)} %cols_hbm.1) | copy-start | bytes 294916

commit v3 on v2

--- a/solution.py
+++ b/solution.py
@@ -145,8 +145,6 @@
             device_id=device(*ROW_SLOTS[at]), device_id_type=MESH,
         )
 
-    square_buf[...] = jnp.zeros_like(square_buf)
-    square_buf[64:72, :] = jnp.ones((8, 128), jnp.float32)
     loads[0].wait()
     for comp in range(3):
         frames = rows_ref[comp]
@@ -157,10 +155,8 @@
         frames = cols_ref[comp]
         cbuf[0, 0, comp * FRAMES:(comp + 1) * FRAMES, :] = frames - jnp.mean(frames, axis=1, keepdims=True)
     loads[2].wait()
-    square_buf[0:64, 0:FRAMES] = vec_ref[...]
-    turned = square_buf[...].T
-    cbuf[0, 0, 96:112, 0:128] = turned[0:16, :]
-    cbuf[0, 0, 96:112, 128:256] = turned[16:32, :]
+    ones = jnp.ones((16, 64), jnp.float32)
+    cbuf[0, 0, 96:112, :] = jnp.concatenate([vec_ref[0:16, :], ones, vec_ref[16:32, :], ones], axis=1)
 
     pl.semaphore_wait(barrier, len(neighbours))
 
@@ -324,8 +320,7 @@
     for at in range(15, 0, -1):
         share_copy(at).wait_recv()
         total = total + landed[at]
-    square_buf[0:FRAMES, :] = total / total[:, 64:65]
-    out_ref[...] = square_buf[...].T[0:64, 0:FRAMES]
+    out_ref[...] = (total / total[:, 64:65])[:, 0:64]
     for at in range(1, 16):
         share_copy(at).wait_send()
 
@@ -336,13 +331,13 @@
     return pl.pallas_call(
         body,
         name="qcp_product",
-        out_shape=jax.ShapeDtypeStruct(vectors.shape, jnp.float32),
-        in_specs=[pl.BlockSpec(memory_space=pl.ANY)] * 3,
+        out_shape=jax.ShapeDtypeStruct(vectors.shape[::-1], jnp.float32),
+        in_specs=[pl.BlockSpec(memory_space=pltpu.HBM)] * 3,
         out_specs=vmem,
         scratch_shapes=[
             pltpu.VMEM(row_frames.shape, jnp.float32),
             pltpu.VMEM(col_frames.shape, jnp.float32),
-            pltpu.VMEM(vectors.shape, jnp.float32),
+            pltpu.VMEM(vectors.shape[::-1], jnp.float32),
             pltpu.VMEM((16, 96, ATOMS), jnp.float32),
             pltpu.VMEM((2, 8, 112, ATOMS), jnp.float32),
             pltpu.VMEM((4, 384, 768), jnp.bfloat16),
@@ -362,9 +357,9 @@
             dma((8, 3)), dma((8, 3)), dma((16,)), dma((16,)),
         ],
         compiler_params=pltpu.CompilerParams(
-            collective_id=0, has_side_effects=True, vmem_limit_bytes=40 << 20,
+            collective_id=0, has_side_effects=True, vmem_limit_bytes=67043328,
         ),
-    )(row_frames, col_frames, vectors)
+    )(row_frames, col_frames, vectors.T).T
 
 
 def solution(mesh):

time: 40 us -> 38.9 us (0.972)
  local copies, waits for them, and re-layouts: 3.26 us -> 1.32 us
  Pallas kernels: 36.5 us -> 37.4 us
    unnamed x5 -> x1, local copies, waits for them, and re-layouts: 2.58 us -> 1.32 us
    pallas_call x1, Pallas kernels: 36.5 us -> 37.4 us  [per_device(): pl.pallas_call(body, name='qcp_product', out_shape=jax.ShapeDtypeStruct(v...]
    pallas_call x1 -> x0, local copies, waits for them, and re-layouts: 0.68 us -> none  [per_device(): pl.pallas_call(body, name='qcp_product', out_shape=jax.ShapeDtypeStruct(v...]
where the time goes in v3:
time: 38.9 us; the launch traced here: 38.7 us
  Pallas kernels  37.4 us (96%)
  local copies, waits for them, and re-layouts  1.32 us (3%)
    pallas_call x1, Pallas kernels, per_device(): pl.pallas_call(body, name='qcp_product', out_shape=jax.ShapeDtypeStruct(v...  37.4 us
    unnamed x1, local copies, waits for them, and re-layouts  1.32 us

profile of v3, /device:TPU:1, one launch (start us, length us, event | category | flops | bytes accessed | tf_op | source)
XLA Modules:
  0.0 38.7 jit_solution(312306218965294847)
XLA Ops:
  0.0 37.4 %qcp_product.1 = f32[32,64]{1,0:T(8,128)} custom-call(f32[3,32,256]{2,1,0:T(8,128)} %rows_hbm.1, f32[3,32,256]{2,1,0:T(8,128)} %cols_hbm.1, f32[32,64]{1,0:T(8,128)} %bitcast.3), custom_call_target="tpu_custom_call" | custom-call | tf_op jit(solution)/shard_map/qcp_product/pallas_call | solution.py:331
  37.4 1.3 %copy.5 = f32[64,32]{0,1:T(8,128)} copy(f32[64,32]{0,1:T(8,128)} %bitcast.2) | data formatting | bytes 16384

commit v4 on v3

--- a/solution.py
+++ b/solution.py
@@ -70,8 +70,8 @@
 COL_PIECES = ((0, 32), (32, 32), (64, 48))
 UNITS = (
     ((0, 0),),
-    ((0, 1), (1, 1), (1, 0)),
-    ((0, 2), (1, 2), (2, 2), (2, 1), (2, 0)),
+    ((1, 0), (1, 1), (0, 1)),
+    ((2, 0), (2, 1), (2, 2), (1, 2), (0, 2)),
     ((3, 0), (3, 1), (3, 2), (3, 3), (2, 3), (1, 3), (0, 3)),
 )
 
@@ -287,24 +287,32 @@
     advance(UNITS[0][0])
     second_round(1)
     second_round(2)
-    settle(((0, 3), (1, 3)), (2, 6))
+    settle(((0, 3), (1, 3)), ())
     prepare_rows(1)
+    advance(UNITS[1][0])
+    third_round(0)
+    settle((), (2, 6))
     prepare_cols(1)
-    for piece in range(3):
-        advance(UNITS[1][piece])
-        third_round(piece)
-    settle(((3, 1), (0, 2), (2, 1)), (3, 5))
+    advance(UNITS[1][1])
+    third_round(1)
+    advance(UNITS[1][2])
+    third_round(2)
+    settle(((3, 1), (0, 2), (2, 1)), ())
     prepare_rows(2)
-    prepare_cols(2)
     for at, unit in enumerate(UNITS[2]):
+        if at == 2:
+            settle((), (3, 5))
+            prepare_cols(2)
         advance(unit)
         if 1 <= at <= 3:
             col_copy(4, at - 1).wait_recv()
             pair_copy(4, at - 1).start()
-    settle(((1, 2), (3, 2), (2, 2)), (0, 4))
+    settle(((1, 2), (3, 2), (2, 2)), ())
     prepare_rows(3)
-    prepare_cols(3)
-    for unit in UNITS[3]:
+    for at, unit in enumerate(UNITS[3]):
+        if at == 3:
+            settle((), (0, 4))
+            prepare_cols(3)
         advance(unit)
     advance(None)
     advance(None)

time: 38.9 us -> 37.5 us (0.964)
  Pallas kernels: 37.4 us -> 36 us
    pallas_call x1, Pallas kernels: 37.4 us -> 36 us  [per_device(): pl.pallas_call(body, name='qcp_product', out_shape=jax.ShapeDtypeStruct(v...]
where the time goes in v4:
time: 37.5 us; the launch traced here: 37.3 us
  Pallas kernels  36 us (96%)
  local copies, waits for them, and re-layouts  1.32 us (4%)
    pallas_call x1, Pallas kernels, per_device(): pl.pallas_call(body, name='qcp_product', out_shape=jax.ShapeDtypeStruct(v...  36 us
    unnamed x1, local copies, waits for them, and re-layouts  1.32 us

profile of v4, /device:TPU:1, one launch (start us, length us, event | category | flops | bytes accessed | tf_op | source)
XLA Modules:
  0.0 37.3 jit_solution(16496594343256848390)
XLA Ops:
  0.0 36.0 %qcp_product.1 = f32[32,64]{1,0:T(8,128)} custom-call(f32[3,32,256]{2,1,0:T(8,128)} %rows_hbm.1, f32[3,32,256]{2,1,0:T(8,128)} %cols_hbm.1, f32[32,64]{1,0:T(8,128)} %bitcast.3), custom_call_target="tpu_custom_call" | custom-call | tf_op jit(solution)/shard_map/qcp_product/pallas_call | solution.py:339
  36.0 1.3 %copy.5 = f32[64,32]{0,1:T(8,128)} copy(f32[64,32]{0,1:T(8,128)} %bitcast.2) | data formatting | bytes 16384

commit v5 on v4

--- a/solution.py
+++ b/solution.py
@@ -66,8 +66,8 @@
     return jnp.exp(jnp.minimum((eigen - full_norm) * (0.5 / ATOMS), 0.0))
 
 
-ROW_PIECES = ((0, 32), (32, 32), (64, 32))
-COL_PIECES = ((0, 32), (32, 32), (64, 48))
+ROW_PIECES = ((0, 48), (48, 48))
+COL_PIECES = ((0, 56), (56, 56))
 UNITS = (
     ((0, 0),),
     ((1, 0), (1, 1), (0, 1)),
@@ -160,7 +160,7 @@
 
     pl.semaphore_wait(barrier, len(neighbours))
 
-    for piece in range(3):
+    for piece in range(2):
         for slot in ((1, 0), (3, 0), (0, 1), (0, 3)):
             row_copy(slot, piece).start()
         col_copy(1, piece).start()
@@ -192,7 +192,7 @@
         pass_on(piece, ((3, 4), (5, None)), (((2, 3), ((2, 2),)),))
 
     def settle(rows, cols):
-        for piece in range(3):
+        for piece in range(2):
             for slot in rows:
                 row_copy(slot, piece).wait_recv()
             for slot in cols:
@@ -278,7 +278,7 @@
             share(valued[0])
         flight["moments"], flight["values"], flight["count"] = unit, ready, count + 1
 
-    for piece in range(3):
+    for piece in range(2):
         first_round(piece)
     settle((), (1, 7))
     prepare_rows(0)
@@ -286,7 +286,6 @@
     second_round(0)
     advance(UNITS[0][0])
     second_round(1)
-    second_round(2)
     settle(((0, 3), (1, 3)), ())
     prepare_rows(1)
     advance(UNITS[1][0])
@@ -296,7 +295,6 @@
     advance(UNITS[1][1])
     third_round(1)
     advance(UNITS[1][2])
-    third_round(2)
     settle(((3, 1), (0, 2), (2, 1)), ())
     prepare_rows(2)
     for at, unit in enumerate(UNITS[2]):
@@ -304,7 +302,7 @@
             settle((), (3, 5))
             prepare_cols(2)
         advance(unit)
-        if 1 <= at <= 3:
+        if 1 <= at <= 2:
             col_copy(4, at - 1).wait_recv()
             pair_copy(4, at - 1).start()
     settle(((1, 2), (3, 2), (2, 2)), ())
@@ -317,7 +315,7 @@
     advance(None)
     advance(None)
 
-    for piece in range(3):
+    for piece in range(2):
         for slot in ROW_SLOTS[1:]:
             row_copy(slot, piece).wait_send()
         for slot in range(1, 8):
@@ -361,8 +359,8 @@
             pltpu.VMEM((16, FRAMES, 128), jnp.float32),
             pltpu.VMEM((16, FRAMES, 128), jnp.float32),
             pltpu.VMEM((128, 128), jnp.float32),
-            dma((3,)), dma((16, 3)), dma((16, 3)), dma((8, 3)), dma((8, 3)),
-            dma((8, 3)), dma((8, 3)), dma((16,)), dma((16,)),
+            dma((3,)), dma((16, 2)), dma((16, 2)), dma((8, 2)), dma((8, 2)),
+            dma((8, 2)), dma((8, 2)), dma((16,)), dma((16,)),
         ],
         compiler_params=pltpu.CompilerParams(
             collective_id=0, has_side_effects=True, vmem_limit_bytes=67043328,

time: 37.5 us -> 36.6 us (0.976)
  Pallas kernels: 36 us -> 35.1 us
    pallas_call x1, Pallas kernels: 36 us -> 35.1 us  [per_device(): pl.pallas_call(body, name='qcp_product', out_shape=jax.ShapeDtypeStruct(v...]
where the time goes in v5:
time: 36.6 us; the launch traced here: 36.4 us
  Pallas kernels  35.1 us (96%)
  local copies, waits for them, and re-layouts  1.32 us (4%)
    pallas_call x1, Pallas kernels, per_device(): pl.pallas_call(body, name='qcp_product', out_shape=jax.ShapeDtypeStruct(v...  35.1 us
    unnamed x1, local copies, waits for them, and re-layouts  1.32 us

profile of v5, /device:TPU:1, one launch (start us, length us, event | category | flops | bytes accessed | tf_op | source)
XLA Modules:
  0.0 36.4 jit_solution(2501769384976583260)
XLA Ops:
  0.0 35.1 %qcp_product.1 = f32[32,64]{1,0:T(8,128)} custom-call(f32[3,32,256]{2,1,0:T(8,128)} %rows_hbm.1, f32[3,32,256]{2,1,0:T(8,128)} %cols_hbm.1, f32[32,64]{1,0:T(8,128)} %bitcast.3), custom_call_target="tpu_custom_call" | custom-call | tf_op jit(solution)/shard_map/qcp_product/pallas_call | solution.py:337
  35.1 1.3 %copy.5 = f32[64,32]{0,1:T(8,128)} copy(f32[64,32]{0,1:T(8,128)} %bitcast.2) | data formatting | bytes 16384

commit v6 on v5

--- a/solution.py
+++ b/solution.py
@@ -168,15 +168,15 @@
         pair_copy(0, piece).start()
 
     def pass_on(piece, cols, rows):
+        for slot, onward in rows:
+            row_copy(slot, piece).wait_recv()
+            for later in onward:
+                row_copy(later, piece).start()
         for slot, onward in cols:
             col_copy(slot, piece).wait_recv()
             if onward is not None:
                 col_copy(onward, piece).start()
             pair_copy(slot, piece).start()
-        for slot, onward in rows:
-            row_copy(slot, piece).wait_recv()
-            for later in onward:
-                row_copy(later, piece).start()
 
     def first_round(piece):
         pass_on(piece, ((1, 2), (7, 6)), (

time: 36.6 us -> 37.7 us (1.030)
  Pallas kernels: 35.1 us -> 36.1 us
    pallas_call x1, Pallas kernels: 35.1 us -> 36.1 us  [per_device(): pl.pallas_call(body, name='qcp_product', out_shape=jax.ShapeDtypeStruct(v...]
where the time goes in v6:
time: 37.7 us; the launch traced here: 37.5 us
  Pallas kernels  36.1 us (96%)
  local copies, waits for them, and re-layouts  1.32 us (4%)
    pallas_call x1, Pallas kernels, per_device(): pl.pallas_call(body, name='qcp_product', out_shape=jax.ShapeDtypeStruct(v...  36.1 us
    unnamed x1, local copies, waits for them, and re-layouts  1.32 us

profile of v6, /device:TPU:1, one launch (start us, length us, event | category | flops | bytes accessed | tf_op | source)
XLA Modules:
  0.0 37.5 jit_solution(3395850773503696189)
XLA Ops:
  0.0 36.1 %qcp_product.1 = f32[32,64]{1,0:T(8,128)} custom-call(f32[3,32,256]{2,1,0:T(8,128)} %rows_hbm.1, f32[3,32,256]{2,1,0:T(8,128)} %cols_hbm.1, f32[32,64]{1,0:T(8,128)} %bitcast.3), custom_call_target="tpu_custom_call" | custom-call | tf_op jit(solution)/shard_map/qcp_product/pallas_call | solution.py:337
  36.2 1.3 %copy.5 = f32[64,32]{0,1:T(8,128)} copy(f32[64,32]{0,1:T(8,128)} %bitcast.2) | data formatting | bytes 16384
